TPU v7x, 32 devices: a whole 2x2x4 slice. The times are simulated.
32 devices in a mesh: ctx: 8 (over y, x, core), qry: 4 (over z).
Axes of the slice: x: 2, y: 2, z: 4, core: 2. Of those that a mesh axis runs over, the one named last changes fastest.
Arguments:
- hist_bins: int32 [512, 16], P(('ctx', 'qry')), may hold values from 0 to 63
- hist_ranks: int32 [512], P(('ctx', 'qry')), may hold values from 0 to 511, each once
- query_bins: int32 [32768, 16], P(('ctx', 'qry')), may hold values from 0 to 63
- bin_table: bfloat16 [1024, 512], replicated, may hold values from -4.5 to 4.5
- rank_vector: bfloat16 [512], replicated, may hold values from -5 to 5
- w_query: bfloat16 [512, 512], replicated, may hold values from -5.833631 to 5.833631
- w_key: bfloat16 [512, 512], replicated, may hold values from -0.176776695 to 0.176776695
- w_value: bfloat16 [512, 512], replicated, may hold values from -0.25 to 0.25
- w_out: bfloat16 [512, 512], replicated, may hold values from -0.25 to 0.25
- w_up: bfloat16 [512, 2048], replicated, may hold values from -0.25 to 0.25
- w_down: bfloat16 [2048, 512], replicated, may hold values from -0.125 to 0.125
Outputs:
- hist_out: bfloat16 [512, 512], P(('ctx', 'qry'))
- query_out: bfloat16 [32768, 512], P(('ctx', 'qry'))
All inputs are finite; a program needn't handle non-finite values.
Results may differ from a plain program's by a relative error of at most 0.008.
Values may be sent and summed in bfloat16 or wider, within the bound.
A program may use at most 64 MiB of HBM per device.

v0:
```python
import jax
import jax.numpy as jnp
from jax import lax
from jax.sharding import PartitionSpec as P

HEADS = 8


epsilon = 1e-05


def passed_along(block, axis, distance):
    devices = range(lax.axis_size(axis))
    route = [((i - distance) % len(devices), i) for i in devices]
    return lax.ppermute(block, axis, route)


def normalize(values):
    centered = values - jnp.mean(values, axis=-1, keepdims=True)
    variance = jnp.mean(centered * centered, axis=-1, keepdims=True)
    return centered * lax.rsqrt(variance + epsilon)


def embed_bins(bin_rows, bin_table):
    bin_count = bin_table.shape[0] // bin_rows.shape[1]
    columns = lax.broadcasted_iota(jnp.int32, (1, bin_count), 1)
    pieces = [
        (bin_rows[:, feature : feature + 1] == columns).astype(jnp.bfloat16)
        for feature in range(bin_rows.shape[1])
    ]
    one_hot = jnp.concatenate(pieces, axis=1)
    return jnp.dot(one_hot, bin_table, preferred_element_type=jnp.float32)


def history_rows(bin_rows, rank_ids, bin_table, rank_vector, history_total):
    level = (2.0 * rank_ids.astype(jnp.float32) + 1.0) / history_total - 1.0
    return (
        embed_bins(bin_rows, bin_table) + level[:, None] * rank_vector.astype(jnp.float32)[None, :]
    )


def pair_move(arrived, offset):
    return passed_along(arrived, "ctx", offset)


def circulate_one(first_block, carry_state, absorb, mover, group_count):

    def advance(step_index, loop_carry):
        moving, current = loop_carry
        moving = mover(moving, 1)
        return (moving, absorb(current, moving))

    return lax.fori_loop(0, group_count - 1, advance, (first_block, carry_state))[1]


def local(
    hist_bins,
    hist_ranks,
    query_bins,
    bin_table,
    rank_vector,
    w_query,
    w_key,
    w_value,
    w_out,
    w_up,
    w_down,
):
    group_count = lax.axis_size("ctx")
    own_rows = hist_bins.shape[0]
    history_total = float(own_rows * group_count * lax.axis_size("qry"))
    own_embed = history_rows(hist_bins, hist_ranks, bin_table, rank_vector, history_total)
    all_rows = jnp.concatenate([own_embed, embed_bins(query_bins, bin_table)], axis=0)
    normed = normalize(all_rows).astype(jnp.bfloat16)
    queries = jnp.dot(normed, w_query, preferred_element_type=jnp.float32).astype(jnp.bfloat16)
    row_count = all_rows.shape[0]
    head_dim = w_query.shape[1] // HEADS
    scale = head_dim ** (-0.5)
    query_heads = queries.reshape(row_count, HEADS, head_dim)
    initial = (
        jnp.full((HEADS, row_count), -1e30, jnp.float32),
        jnp.zeros((HEADS, row_count), jnp.float32),
        jnp.zeros((HEADS, row_count, head_dim), jnp.float32),
    )

    def absorb_pair(carry_state, key_rows, value_rows):
        row_peak, row_total, summed = carry_state
        key_heads = key_rows.reshape(-1, HEADS, head_dim)
        value_heads = value_rows.reshape(-1, HEADS, head_dim)
        scores = (
            jnp.einsum("nhd,khd->hnk", query_heads, key_heads, preferred_element_type=jnp.float32)
            * scale
        )
        new_peak = jnp.maximum(row_peak, jnp.max(scores, axis=-1))
        factor = jnp.exp(row_peak - new_peak)
        weights = jnp.exp(scores - new_peak[..., None])
        row_total = row_total * factor + jnp.sum(weights, axis=-1)
        summed = summed * factor[..., None] + jnp.einsum(
            "hnk,khd->hnd",
            weights.astype(jnp.bfloat16),
            value_heads,
            preferred_element_type=jnp.float32,
        )
        return (new_peak, row_total, summed)

    history_normed = normed[:own_rows]
    key_rows = jnp.dot(history_normed, w_key, preferred_element_type=jnp.float32).astype(
        jnp.bfloat16
    )
    value_rows = jnp.dot(history_normed, w_value, preferred_element_type=jnp.float32).astype(
        jnp.bfloat16
    )
    key_pairs = jnp.stack((key_rows, value_rows))
    first_block = lax.all_gather(key_pairs, "qry", axis=1, tiled=True)

    def absorb(carry_state, arrived):
        return absorb_pair(carry_state, arrived[0], arrived[1])

    carry_state = absorb(initial, first_block)
    carry_state = circulate_one(first_block, carry_state, absorb, pair_move, group_count)
    row_peak, row_total, summed = carry_state
    attended = (
        jnp.transpose(summed / row_total[..., None], (1, 0, 2))
        .reshape(row_count, -1)
        .astype(jnp.bfloat16)
    )
    after_attention = all_rows + jnp.dot(attended, w_out, preferred_element_type=jnp.float32)
    inner = jnp.dot(
        normalize(after_attention).astype(jnp.bfloat16), w_up, preferred_element_type=jnp.float32
    )
    hidden = jax.nn.gelu(inner, approximate=True).astype(jnp.bfloat16)
    result = (after_attention + jnp.dot(hidden, w_down, preferred_element_type=jnp.float32)).astype(
        jnp.bfloat16
    )
    return (result[:own_rows], result[own_rows:])


def solution(mesh):
    return jax.shard_map(
        local,
        mesh=mesh,
        in_specs=(
            P(("ctx", "qry"), None),
            P(("ctx", "qry")),
            P(("ctx", "qry"), None),
            P(),
            P(),
            P(),
            P(),
            P(),
            P(),
            P(),
            P(),
        ),
        out_specs=(P(("ctx", "qry"), None), P(("ctx", "qry"), None)),
        check_vma=False,
    )
```

profile of v0, /device:TPU:0, one launch (start us, length us, event | category | flops | bytes accessed | tf_op | source)
XLA Modules:
  0.0 152.9 jit_solution(12912885577135275044)
XLA Ops:
  2.1 1.7 %slice_reduce_fusion = (s32[16]{0:T(128)S(1)}, s32[16]{0:T(128)S(1)}, s32[16]{0:T(128)S(1)}, s32[16]{0:T(128)S(1)}, s32[16]{0:T(128)S(1)}, /*index=5*/s32[16]{0:...) fusion(s32[16,16]{1,0:T(8,128)} %param.13), kind=kLoop, calls=%fused_computation.67 | loop fusion | bytes 2048 | tf_op jit(solution)/shard_map/slice | solution.py:28
  4.6 1.5 convolution_add_fusion.4
  6.1 1.3 fusion.36
  7.7 1.0 iota_compare_fusion
  8.8 1.0 iota_compare_fusion.4
  9.8 1.0 iota_compare_fusion.6
  10.9 1.0 iota_compare_fusion.8
  11.9 1.0 iota_compare_fusion.10
  12.9 1.0 iota_compare_fusion.12
  14.0 1.0 iota_compare_fusion.14
  15.0 5.7 %concatenate.17 = pred[1024,1024]{1,0:T(32,128)(4,1)S(1)} concatenate(pred[1024,64]{1,0:T(32,128)(4,1)} %get-tuple-element.116, pred[1024,64]{1,0:T(32,128)(4,1)} %get-tuple-element.115, pred[1024,64]{1,0:T(32,128)(4,1)} %get-tuple-element.114, pred[1024,64]{1,0:T(32,128)(4,1)} %get-tuple-element.113, pred[1024,64]{1,0:T(32,128)(4,1)} %get-tuple-element.112, ...), dimensions={1} | concatenate | bytes 2097152 | tf_op jit(solution)/shard_map/concatenate | solution.py:31
  20.7 2.5 %fusion.39 = f32[1024,512]{1,0:T(8,128)S(1)} fusion(pred[1024,1024]{1,0:T(32,128)(4,1)S(1)} %concatenate.17, bf16[1024,512]{1,0:T(8,128)(2,1)} %param.16), kind=kOutput, calls=%fused_computation.112 | convolution fusion | flops 1073741824 | bytes 4194304 | tf_op jit(solution)/shard_map/dot_general | solution.py:32
  25.6 1.7 %convolution_convert_fusion = bf16[1040,512]{1,0:T(8,128)(2,1)} fusion(bf16[1040,512]{1,0:T(8,128)(2,1)S(1)} %multiply_convert_fusion.1, bf16[512,512]{1,0:T(8,128)(2,1)S(1)} %copy-done.19), kind=kOutput, calls=%fused_computation.23 | convolution fusion | flops 545792000 | bytes 2654208 | tf_op jit(solution)/shard_map/dot_general | solution.py:75
  27.3 15.2 %all_gather.3 = bf16[2,64,512]{2,1,0:T(8,128)(2,1)S(1)} all-gather(bf16[2,16,512]{2,1,0:T(8,128)(2,1)S(1)} %pad_maximum_fusion.1), channel_id=1, replica_groups=mesh['ctx'=8,'qry'=4] {'qry'}, dimensions={1}, use_global_device_ids=true | all-gather | bytes 163840 | tf_op jit(solution)/shard_map/all_gather | solution.py:114
  42.5 1.7 %copy.20 = bf16[1040,512]{0,1:T(8,128)(2,1)S(1)} copy(bf16[1040,512]{1,0:T(8,128)(2,1)} %convolution_convert_fusion) | data formatting | bytes 2129920 | tf_op jit(solution)/shard_map/convert_element_type | solution.py:75
  45.0 1.0 reshape_squeeze.6
  47.5 1.9 %convolution_add_fusion.2 = f32[8,1040,64]{1,2,0:T(8,128)} fusion(bf16[64,8,64]{0,2,1:T(8,128)(2,1)S(1)} %bitcast.52, f32[8,1040,64]{1,2,0:T(8,128)S(1)} %get-tuple-element.98, f32[8,1040]{1,0:T(8,128)S(1)} %get-tuple-element.95, f32[8,1040]{1,0:T(8,128)S(1)} %broadcast_maximum_fusion), kind=kOutput, calls=%fused_computation.19 | convolution fusion | flops 69754880 | bytes 4391936 | tf_op jit(solution)/shard_map/hnk,khd->hnd/dot_general | solution.py:98
  49.4 88.3 %while.16 = (s32[]{:T(128)}, bf16[2,64,512]{2,1,0:T(8,128)(2,1)S(1)}, f32[8,1040]{1,0:T(8,128)}, f32[8,1040]{1,0:T(8,128)}, f32[8,1040,64]{1,2,0:T(8,128)}, /*index=5*/bf16[1040,8,64]{0,2,1:T(8,128)(2,1)S(1)}, s32[]{:T(128)}) while((s32[]{:T(128)}, bf16[2,64,512]{2,1,0:T(8,128)(2,1)S(1)}, f32[8,1040]{1,0:T(8,128)}, f32[8,1040]{1,0:T(8,128)}, ...), condition=%wide.region_7.0_spmd, body=%wide.region_4.0_spmd.sunk | while | flops 140591360 | bytes 32176440 | solution.py:53
  49.4 5.3 %collective-permute-done = bf16[2,64,512]{2,1,0:T(8,128)(2,1)S(1)} collective-permute-done((bf16[2,64,512]{2,1,0:T(8,128)(2,1)S(1)}, bf16[2,64,512]{2,1,0:T(8,128)(2,1)S(1)}, u32[]{:S(2)}, u32[]{:S(2)}) %collective-permute-start) | collective-permute-done | bytes 131104 | tf_op jit(solution)/shard_map/while/body/eval_jaxpr/ppermute | solution.py:15
  55.4 1.0 squeeze.7
  59.6 1.1 convolution_add_fusion.6
  60.7 1.4 copy-done.2
  62.1 5.3 %collective-permute-done = bf16[2,64,512]{2,1,0:T(8,128)(2,1)S(1)} collective-permute-done((bf16[2,64,512]{2,1,0:T(8,128)(2,1)S(1)}, bf16[2,64,512]{2,1,0:T(8,128)(2,1)S(1)}, u32[]{:S(2)}, u32[]{:S(2)}) %collective-permute-start) | collective-permute-done | bytes 131104 | tf_op jit(solution)/shard_map/while/body/eval_jaxpr/ppermute | solution.py:15
  68.0 1.0 squeeze.7
  72.2 1.1 convolution_add_fusion.6
  73.3 1.4 copy-done.2
  74.7 5.3 %collective-permute-done = bf16[2,64,512]{2,1,0:T(8,128)(2,1)S(1)} collective-permute-done((bf16[2,64,512]{2,1,0:T(8,128)(2,1)S(1)}, bf16[2,64,512]{2,1,0:T(8,128)(2,1)S(1)}, u32[]{:S(2)}, u32[]{:S(2)}) %collective-permute-start) | collective-permute-done | bytes 131104 | tf_op jit(solution)/shard_map/while/body/eval_jaxpr/ppermute | solution.py:15
  80.6 1.0 squeeze.7
  84.8 1.1 convolution_add_fusion.6
  85.9 1.4 copy-done.2
  87.3 5.3 %collective-permute-done = bf16[2,64,512]{2,1,0:T(8,128)(2,1)S(1)} collective-permute-done((bf16[2,64,512]{2,1,0:T(8,128)(2,1)S(1)}, bf16[2,64,512]{2,1,0:T(8,128)(2,1)S(1)}, u32[]{:S(2)}, u32[]{:S(2)}) %collective-permute-start) | collective-permute-done | bytes 131104 | tf_op jit(solution)/shard_map/while/body/eval_jaxpr/ppermute | solution.py:15
  93.2 1.0 squeeze.7
  97.4 1.1 convolution_add_fusion.6
  98.5 1.4 copy-done.2
  99.9 5.3 %collective-permute-done = bf16[2,64,512]{2,1,0:T(8,128)(2,1)S(1)} collective-permute-done((bf16[2,64,512]{2,1,0:T(8,128)(2,1)S(1)}, bf16[2,64,512]{2,1,0:T(8,128)(2,1)S(1)}, u32[]{:S(2)}, u32[]{:S(2)}) %collective-permute-start) | collective-permute-done | bytes 131104 | tf_op jit(solution)/shard_map/while/body/eval_jaxpr/ppermute | solution.py:15
  105.9 1.0 squeeze.7
  110.0 1.1 convolution_add_fusion.6
  111.1 1.4 copy-done.2
  112.5 5.3 %collective-permute-done = bf16[2,64,512]{2,1,0:T(8,128)(2,1)S(1)} collective-permute-done((bf16[2,64,512]{2,1,0:T(8,128)(2,1)S(1)}, bf16[2,64,512]{2,1,0:T(8,128)(2,1)S(1)}, u32[]{:S(2)}, u32[]{:S(2)}) %collective-permute-start) | collective-permute-done | bytes 131104 | tf_op jit(solution)/shard_map/while/body/eval_jaxpr/ppermute | solution.py:15
  122.6 1.1 convolution_add_fusion.6
  123.7 1.4 copy-done.2
  125.1 5.3 %collective-permute-done = bf16[2,64,512]{2,1,0:T(8,128)(2,1)S(1)} collective-permute-done((bf16[2,64,512]{2,1,0:T(8,128)(2,1)S(1)}, bf16[2,64,512]{2,1,0:T(8,128)(2,1)S(1)}, u32[]{:S(2)}, u32[]{:S(2)}) %collective-permute-start) | collective-permute-done | bytes 131104 | tf_op jit(solution)/shard_map/while/body/eval_jaxpr/ppermute | solution.py:15
  135.2 1.1 convolution_add_fusion.6
  136.3 1.4 copy-done.2
  137.7 2.0 %divide_convert_fusion = bf16[8,1040,64]{1,2,0:T(8,128)(2,1)S(1)} fusion(f32[8,1040,64]{1,2,0:T(8,128)} %get-tuple-element.35, f32[8,1040]{1,0:T(8,128)} %get-tuple-element.36), kind=kLoop, calls=%fused_computation.24 | loop fusion | flops 1064960 | bytes 3228160 | tf_op jit(solution)/shard_map/convert_element_type | solution.py:125
  141.0 1.3 copy-done.7
  142.8 8.4 %fusion.13 = bf16[1040,512]{1,0:T(8,128)(2,1)S(1)} fusion(f32[1040,512]{1,0:T(8,128)} %copy-done.7, bf16[2048,512]{1,0:T(8,128)(2,1)S(1)} %copy-done, bf16[512,2048]{1,0:T(8,128)(2,1)} %param.22, f32[1040]{0:T(1024)S(1)} %add_rsqrt_fusion, f32[1040]{0:T(1024)S(1)} %broadcast_multiply_fusion), kind=kOutput, calls=%fused_computation.22 | convolution fusion | flops 4383907840 | bytes 7397504 | tf_op jit(solution)/shard_map/dot_general | solution.py:132
  151.8 1.0 slice.160
  (212 shorter events, 38.0 us)
Async XLA Ops:
  0.6 142.2 %copy-start = (bf16[2048,512]{1,0:T(8,128)(2,1)S(1)}, bf16[2048,512]{1,0:T(8,128)(2,1)}, u32[]{:S(2)}) copy-start(bf16[2048,512]{1,0:T(8,128)(2,1)} %param.23) | copy-start | bytes 6291460
  6.1 17.9 %copy-start.12 = (f32[16,512]{1,0:T(8,128)}, f32[16,512]{1,0:T(8,128)S(1)}, u32[]{:S(2)}) copy-start(f32[16,512]{1,0:T(8,128)S(1)} %convolution_add_fusion.4) | copy-start | bytes 98308
  23.2 1.3 copy-start.3
  23.9 1.2 copy-start.18
  24.5 1.1 copy-start.19
  42.5 2.3 %copy-start.15 = (bf16[2,64,512]{2,1,0:T(8,128)(2,1)}, bf16[2,64,512]{2,1,0:T(8,128)(2,1)S(1)}, u32[]{:S(2)}) copy-start(bf16[2,64,512]{2,1,0:T(8,128)(2,1)S(1)} %all_gather.3) | copy-start | bytes 393220
  46.5 3.0 %copy-start.8 = (f32[8,1040]{1,0:T(8,128)}, f32[8,1040]{1,0:T(8,128)S(1)}, u32[]{:S(2)}) copy-start(f32[8,1040]{1,0:T(8,128)S(1)} %broadcast_maximum_fusion) | copy-start | bytes 99844
  47.5 1.9 %copy-start.16 = (bf16[2,64,512]{2,1,0:T(8,128)(2,1)S(1)}, bf16[2,64,512]{2,1,0:T(8,128)(2,1)}, u32[]{:S(2)}) copy-start(bf16[2,64,512]{2,1,0:T(8,128)(2,1)} %copy-done.15) | copy-start | bytes 393220
  49.4 5.3 %collective-permute-start = (bf16[2,64,512]{2,1,0:T(8,128)(2,1)S(1)}, bf16[2,64,512]{2,1,0:T(8,128)(2,1)S(1)}, u32[]{:S(2)}, u32[]{:S(2)}) collective-permute-start(bf16[2,64,512]{2,1,0:T(8,128)(2,1)S(1)} %get-tuple-element.190), channel_id=1, source_target_pairs={{28,0},{0,4},{4,8},{8,12},{12,16},{16,20},{20,24},{24,28},{29,1},{... | collective-permute-start | bytes 393224 | tf_op jit(solution)/shard_map/while/body/eval_jaxpr/ppermute | solution.py:15
  54.7 1.7 %copy-start.5 = (bf16[2,64,512]{2,1,0:T(8,128)(2,1)}, bf16[2,64,512]{2,1,0:T(8,128)(2,1)S(1)}, u32[]{:S(2)}) copy-start(bf16[2,64,512]{2,1,0:T(8,128)(2,1)S(1)} %collective-permute-done) | copy-start | bytes 393220 | tf_op jit(solution)/shard_map/while
  57.9 1.7 %copy-start.1 = (f32[8,1040,64]{1,2,0:T(8,128)S(1)}, f32[8,1040,64]{1,2,0:T(8,128)}, u32[]{:S(2)}) copy-start(f32[8,1040,64]{1,2,0:T(8,128)} %get-tuple-element.193) | copy-start | bytes 6389764 | tf_op jit(solution)/shard_map/while
  58.7 2.0 %copy-start.11 = (f32[8,1040]{1,0:T(8,128)}, f32[8,1040]{1,0:T(8,128)S(1)}, u32[]{:S(2)}) copy-start(f32[8,1040]{1,0:T(8,128)S(1)} %get-tuple-element.199) | copy-start | bytes 99844 | tf_op jit(solution)/shard_map/while
  59.5 1.1 copy-start.6
  60.6 1.4 copy-start.2
  62.1 5.3 %collective-permute-start = (bf16[2,64,512]{2,1,0:T(8,128)(2,1)S(1)}, bf16[2,64,512]{2,1,0:T(8,128)(2,1)S(1)}, u32[]{:S(2)}, u32[]{:S(2)}) collective-permute-start(bf16[2,64,512]{2,1,0:T(8,128)(2,1)S(1)} %get-tuple-element.190), channel_id=1, source_target_pairs={{28,0},{0,4},{4,8},{8,12},{12,16},{16,20},{20,24},{24,28},{29,1},{... | collective-permute-start | bytes 393224 | tf_op jit(solution)/shard_map/while/body/eval_jaxpr/ppermute | solution.py:15
  67.4 1.7 %copy-start.5 = (bf16[2,64,512]{2,1,0:T(8,128)(2,1)}, bf16[2,64,512]{2,1,0:T(8,128)(2,1)S(1)}, u32[]{:S(2)}) copy-start(bf16[2,64,512]{2,1,0:T(8,128)(2,1)S(1)} %collective-permute-done) | copy-start | bytes 393220 | tf_op jit(solution)/shard_map/while
  70.5 1.7 %copy-start.1 = (f32[8,1040,64]{1,2,0:T(8,128)S(1)}, f32[8,1040,64]{1,2,0:T(8,128)}, u32[]{:S(2)}) copy-start(f32[8,1040,64]{1,2,0:T(8,128)} %get-tuple-element.193) | copy-start | bytes 6389764 | tf_op jit(solution)/shard_map/while
  71.3 2.0 %copy-start.11 = (f32[8,1040]{1,0:T(8,128)}, f32[8,1040]{1,0:T(8,128)S(1)}, u32[]{:S(2)}) copy-start(f32[8,1040]{1,0:T(8,128)S(1)} %get-tuple-element.199) | copy-start | bytes 99844 | tf_op jit(solution)/shard_map/while
  73.3 1.4 copy-start.2
  74.7 5.3 %collective-permute-start = (bf16[2,64,512]{2,1,0:T(8,128)(2,1)S(1)}, bf16[2,64,512]{2,1,0:T(8,128)(2,1)S(1)}, u32[]{:S(2)}, u32[]{:S(2)}) collective-permute-start(bf16[2,64,512]{2,1,0:T(8,128)(2,1)S(1)} %get-tuple-element.190), channel_id=1, source_target_pairs={{28,0},{0,4},{4,8},{8,12},{12,16},{16,20},{20,24},{24,28},{29,1},{... | collective-permute-start | bytes 393224 | tf_op jit(solution)/shard_map/while/body/eval_jaxpr/ppermute | solution.py:15
  80.0 1.7 %copy-start.5 = (bf16[2,64,512]{2,1,0:T(8,128)(2,1)}, bf16[2,64,512]{2,1,0:T(8,128)(2,1)S(1)}, u32[]{:S(2)}) copy-start(bf16[2,64,512]{2,1,0:T(8,128)(2,1)S(1)} %collective-permute-done) | copy-start | bytes 393220 | tf_op jit(solution)/shard_map/while
  83.1 1.7 %copy-start.1 = (f32[8,1040,64]{1,2,0:T(8,128)S(1)}, f32[8,1040,64]{1,2,0:T(8,128)}, u32[]{:S(2)}) copy-start(f32[8,1040,64]{1,2,0:T(8,128)} %get-tuple-element.193) | copy-start | bytes 6389764 | tf_op jit(solution)/shard_map/while
  83.9 2.0 %copy-start.11 = (f32[8,1040]{1,0:T(8,128)}, f32[8,1040]{1,0:T(8,128)S(1)}, u32[]{:S(2)}) copy-start(f32[8,1040]{1,0:T(8,128)S(1)} %get-tuple-element.199) | copy-start | bytes 99844 | tf_op jit(solution)/shard_map/while
  85.9 1.4 copy-start.2
  87.3 5.3 %collective-permute-start = (bf16[2,64,512]{2,1,0:T(8,128)(2,1)S(1)}, bf16[2,64,512]{2,1,0:T(8,128)(2,1)S(1)}, u32[]{:S(2)}, u32[]{:S(2)}) collective-permute-start(bf16[2,64,512]{2,1,0:T(8,128)(2,1)S(1)} %get-tuple-element.190), channel_id=1, source_target_pairs={{28,0},{0,4},{4,8},{8,12},{12,16},{16,20},{20,24},{24,28},{29,1},{... | collective-permute-start | bytes 393224 | tf_op jit(solution)/shard_map/while/body/eval_jaxpr/ppermute | solution.py:15
  92.6 1.7 %copy-start.5 = (bf16[2,64,512]{2,1,0:T(8,128)(2,1)}, bf16[2,64,512]{2,1,0:T(8,128)(2,1)S(1)}, u32[]{:S(2)}) copy-start(bf16[2,64,512]{2,1,0:T(8,128)(2,1)S(1)} %collective-permute-done) | copy-start | bytes 393220 | tf_op jit(solution)/shard_map/while
  95.7 1.7 %copy-start.1 = (f32[8,1040,64]{1,2,0:T(8,128)S(1)}, f32[8,1040,64]{1,2,0:T(8,128)}, u32[]{:S(2)}) copy-start(f32[8,1040,64]{1,2,0:T(8,128)} %get-tuple-element.193) | copy-start | bytes 6389764 | tf_op jit(solution)/shard_map/while
  96.5 2.0 %copy-start.11 = (f32[8,1040]{1,0:T(8,128)}, f32[8,1040]{1,0:T(8,128)S(1)}, u32[]{:S(2)}) copy-start(f32[8,1040]{1,0:T(8,128)S(1)} %get-tuple-element.199) | copy-start | bytes 99844 | tf_op jit(solution)/shard_map/while
  98.5 1.4 copy-start.2
  99.9 5.3 %collective-permute-start = (bf16[2,64,512]{2,1,0:T(8,128)(2,1)S(1)}, bf16[2,64,512]{2,1,0:T(8,128)(2,1)S(1)}, u32[]{:S(2)}, u32[]{:S(2)}) collective-permute-start(bf16[2,64,512]{2,1,0:T(8,128)(2,1)S(1)} %get-tuple-element.190), channel_id=1, source_target_pairs={{28,0},{0,4},{4,8},{8,12},{12,16},{16,20},{20,24},{24,28},{29,1},{... | collective-permute-start | bytes 393224 | tf_op jit(solution)/shard_map/while/body/eval_jaxpr/ppermute | solution.py:15
  105.2 1.7 %copy-start.5 = (bf16[2,64,512]{2,1,0:T(8,128)(2,1)}, bf16[2,64,512]{2,1,0:T(8,128)(2,1)S(1)}, u32[]{:S(2)}) copy-start(bf16[2,64,512]{2,1,0:T(8,128)(2,1)S(1)} %collective-permute-done) | copy-start | bytes 393220 | tf_op jit(solution)/shard_map/while
  108.3 1.7 %copy-start.1 = (f32[8,1040,64]{1,2,0:T(8,128)S(1)}, f32[8,1040,64]{1,2,0:T(8,128)}, u32[]{:S(2)}) copy-start(f32[8,1040,64]{1,2,0:T(8,128)} %get-tuple-element.193) | copy-start | bytes 6389764 | tf_op jit(solution)/shard_map/while
  109.1 2.0 %copy-start.11 = (f32[8,1040]{1,0:T(8,128)}, f32[8,1040]{1,0:T(8,128)S(1)}, u32[]{:S(2)}) copy-start(f32[8,1040]{1,0:T(8,128)S(1)} %get-tuple-element.199) | copy-start | bytes 99844 | tf_op jit(solution)/shard_map/while
  111.1 1.4 copy-start.2
  112.5 5.3 %collective-permute-start = (bf16[2,64,512]{2,1,0:T(8,128)(2,1)S(1)}, bf16[2,64,512]{2,1,0:T(8,128)(2,1)S(1)}, u32[]{:S(2)}, u32[]{:S(2)}) collective-permute-start(bf16[2,64,512]{2,1,0:T(8,128)(2,1)S(1)} %get-tuple-element.190), channel_id=1, source_target_pairs={{28,0},{0,4},{4,8},{8,12},{12,16},{16,20},{20,24},{24,28},{29,1},{... | collective-permute-start | bytes 393224 | tf_op jit(solution)/shard_map/while/body/eval_jaxpr/ppermute | solution.py:15
  117.8 1.7 %copy-start.5 = (bf16[2,64,512]{2,1,0:T(8,128)(2,1)}, bf16[2,64,512]{2,1,0:T(8,128)(2,1)S(1)}, u32[]{:S(2)}) copy-start(bf16[2,64,512]{2,1,0:T(8,128)(2,1)S(1)} %collective-permute-done) | copy-start | bytes 393220 | tf_op jit(solution)/shard_map/while
  120.9 1.7 %copy-start.1 = (f32[8,1040,64]{1,2,0:T(8,128)S(1)}, f32[8,1040,64]{1,2,0:T(8,128)}, u32[]{:S(2)}) copy-start(f32[8,1040,64]{1,2,0:T(8,128)} %get-tuple-element.193) | copy-start | bytes 6389764 | tf_op jit(solution)/shard_map/while
  121.7 2.0 %copy-start.11 = (f32[8,1040]{1,0:T(8,128)}, f32[8,1040]{1,0:T(8,128)S(1)}, u32[]{:S(2)}) copy-start(f32[8,1040]{1,0:T(8,128)S(1)} %get-tuple-element.199) | copy-start | bytes 99844 | tf_op jit(solution)/shard_map/while
  123.7 1.4 copy-start.2
  125.1 5.3 %collective-permute-start = (bf16[2,64,512]{2,1,0:T(8,128)(2,1)S(1)}, bf16[2,64,512]{2,1,0:T(8,128)(2,1)S(1)}, u32[]{:S(2)}, u32[]{:S(2)}) collective-permute-start(bf16[2,64,512]{2,1,0:T(8,128)(2,1)S(1)} %get-tuple-element.190), channel_id=1, source_target_pairs={{28,0},{0,4},{4,8},{8,12},{12,16},{16,20},{20,24},{24,28},{29,1},{... | collective-permute-start | bytes 393224 | tf_op jit(solution)/shard_map/while/body/eval_jaxpr/ppermute | solution.py:15
  130.4 1.7 %copy-start.5 = (bf16[2,64,512]{2,1,0:T(8,128)(2,1)}, bf16[2,64,512]{2,1,0:T(8,128)(2,1)S(1)}, u32[]{:S(2)}) copy-start(bf16[2,64,512]{2,1,0:T(8,128)(2,1)S(1)} %collective-permute-done) | copy-start | bytes 393220 | tf_op jit(solution)/shard_map/while
  133.5 1.7 %copy-start.1 = (f32[8,1040,64]{1,2,0:T(8,128)S(1)}, f32[8,1040,64]{1,2,0:T(8,128)}, u32[]{:S(2)}) copy-start(f32[8,1040,64]{1,2,0:T(8,128)} %get-tuple-element.193) | copy-start | bytes 6389764 | tf_op jit(solution)/shard_map/while
  134.3 2.0 %copy-start.11 = (f32[8,1040]{1,0:T(8,128)}, f32[8,1040]{1,0:T(8,128)S(1)}, u32[]{:S(2)}) copy-start(f32[8,1040]{1,0:T(8,128)S(1)} %get-tuple-element.199) | copy-start | bytes 99844 | tf_op jit(solution)/shard_map/while
  136.3 1.4 copy-start.2
  137.7 2.3 %copy-start.4 = (f32[1024,512]{1,0:T(8,128)S(1)}, f32[1024,512]{1,0:T(8,128)}, u32[]{:S(2)}) copy-start(f32[1024,512]{1,0:T(8,128)} %copy-done.3) | copy-start | bytes 6291460
  137.7 2.3 %copy-start.13 = (f32[16,512]{1,0:T(8,128)S(1)}, f32[16,512]{1,0:T(8,128)}, u32[]{:S(2)}) copy-start(f32[16,512]{1,0:T(8,128)} %copy-done.12) | copy-start | bytes 98308
  137.7 2.4 %copy-start.14 = (bf16[512,512]{1,0:T(8,128)(2,1)S(1)}, bf16[512,512]{1,0:T(8,128)(2,1)}, u32[]{:S(2)}) copy-start(bf16[512,512]{1,0:T(8,128)(2,1)} %param.21) | copy-start | bytes 1572868
  141.0 1.4 copy-start.7
  (21 other events, 18.4 us)
where the time goes:
time: 155 us; the launch traced here: 153 us
  local copies, waits for them, and re-layouts  53.6 us (35%)
  waiting for transfers between devices  37 us (24%)
  matrix products  28.3 us (18%)
  other arithmetic  17.1 us (11%)
  blocking collectives  15.2 us (10%)
    ppermute x7, waiting for transfers between devices, passed_along(): return lax.ppermute(block, axis, route)  37 us
    while x112, local copies, waits for them, and re-layouts  18.7 us
    all_gather x1, blocking collectives, local(): first_block = lax.all_gather(key_pairs, 'qry', axis=1, tiled=True)  15.2 us
    slice x15, local copies, waits for them, and re-layouts, absorb(): return absorb_pair(carry_state, arrived[0], arrived[1])  12.1 us
    dot_general x8, matrix products, absorb_pair(): jnp.einsum('hnk,khd->hnd', weights.astype(jnp.bfloat16), value_heads, pre...  9.39 us
    dot_general x1, matrix products, local(): jnp.dot(hidden, w_down, preferred_element_type=jnp.float32)  8.4 us
    eq x16, other arithmetic, embed_bins(): bin_rows[:, feature:feature + 1] == columns  8.22 us
    squeeze x7, local copies, waits for them, and re-layouts, absorb_pair(): key_heads = key_rows.reshape(-1, HEADS, head_dim)  6.83 us
  transfers between devices with their start and end apart: 7, of which 7 were waited for; matrix products, arithmetic and copies ran while one was open for 0% of the time, Pallas kernels for 0%

commit v1 on v0

v1 whole, which is shorter than its diff:
```python
import functools
import math

import jax
import jax.numpy as jnp
from jax import lax
from jax.experimental import pallas as pl
from jax.experimental.pallas import tpu as pltpu
from jax.sharding import PartitionSpec as P

HEADS = 8
LANES = 128
RADIX = 64
epsilon = 1e-05
F32 = jnp.float32
BF16 = jnp.bfloat16


def normalize(values):
    centered = values - jnp.mean(values, axis=-1, keepdims=True)
    variance = jnp.mean(centered * centered, axis=-1, keepdims=True)
    return centered * lax.rsqrt(variance + epsilon)


def dot(a, b):
    return jnp.dot(a, b, preferred_element_type=F32)


def embed(bins, spread, column_bin, table):
    named = dot(bins, spread)
    one_hot = jnp.where(named == column_bin, 1.0, 0.0).astype(BF16)
    return dot(one_hot, table)


def embed_kernel(
    sizes,
    query_bins,
    hist_bins,
    hist_ranks,
    table,
    rank_vector,
    w_query,
    w_key,
    w_value,
    rows_out,
    queries_out,
    keys_out,
    values_out,
    staged,
    mine,
    blocks,
    hist_rows,
    hist_normed,
    send_sem,
    recv_sem,
):
    inner, count, query_tile, hist_tile = sizes
    own, features = hist_bins.shape
    query_count = query_bins.shape[0]
    total = count * own
    me = lax.axis_index("ctx") * inner + lax.axis_index("qry")

    def place(index):
        return {"ctx": index // inner, "qry": index % inner}

    def partner(step):
        return (me + step) % count

    barrier = pltpu.get_barrier_semaphore()

    def greet(step, carry):
        pl.semaphore_signal(
            barrier,
            inc=1,
            device_id=place(partner(step)),
            device_id_type=pl.DeviceIdType.MESH,
        )
        return carry

    lax.fori_loop(1, count, greet, 0)

    ranks = jnp.broadcast_to(hist_ranks[...], (own, own))
    diagonal = lax.broadcasted_iota(jnp.int32, (own, own), 0) == lax.broadcasted_iota(
        jnp.int32, (own, own), 1
    )
    rank = jnp.sum(jnp.where(diagonal, ranks.astype(F32), 0.0), axis=1, keepdims=True)
    high = jnp.floor(rank * (1.0 / RADIX))
    staged[...] = jnp.zeros_like(staged)
    staged[:, :features] = hist_bins[...].astype(F32)
    staged[:, features : features + 1] = high
    staged[:, features + 1 : features + 2] = rank - high * RADIX
    mine[...] = staged[...].astype(BF16)
    blocks[me] = mine[...]

    bin_count = table.shape[0] // features
    wide = (features, table.shape[0])
    spread = jnp.where(
        lax.broadcasted_iota(jnp.int32, wide, 1) // bin_count
        == lax.broadcasted_iota(jnp.int32, wide, 0),
        1.0,
        0.0,
    ).astype(BF16)
    column_bin = (
        lax.broadcasted_iota(jnp.int32, (1, table.shape[0]), 1) % bin_count
    ).astype(F32)

    def copy_to(step):
        other = partner(step)
        return pltpu.make_async_remote_copy(
            src_ref=mine,
            dst_ref=blocks.at[me],
            send_sem=send_sem.at[other],
            recv_sem=recv_sem.at[me],
            device_id=place(other),
            device_id_type=pl.DeviceIdType.MESH,
        )

    def copy_from(step):
        other = partner(step)
        return pltpu.make_async_remote_copy(
            src_ref=mine,
            dst_ref=blocks.at[other],
            send_sem=send_sem.at[other],
            recv_sem=recv_sem.at[other],
            device_id=place(other),
            device_id_type=pl.DeviceIdType.MESH,
        )

    def send(step, carry):
        copy_to(step).start()
        return carry

    pl.semaphore_wait(barrier, count - 1)
    lax.fori_loop(1, count, send, 0)

    def query_step(index, carry):
        at = pl.ds(pl.multiple_of(index * query_tile, query_tile), query_tile)
        found = embed(query_bins[at, :].astype(F32).astype(BF16), spread, column_bin, table[...])
        rows_out[at, :] = found
        queries_out[at, :] = dot(normalize(found).astype(BF16), w_query[...]).astype(BF16)
        return carry

    lax.fori_loop(0, query_count // query_tile, query_step, 0)

    def finish(step, carry):
        copy_to(step).wait_send()
        copy_from(step).wait_recv()
        return carry

    lax.fori_loop(1, count, finish, 0)

    def hist_step(index, carry):
        tile_blocks = hist_tile // own
        block = blocks[pl.ds(index * tile_blocks, tile_blocks)].reshape(hist_tile, LANES)
        at = pl.ds(pl.multiple_of(index * hist_tile, hist_tile), hist_tile)
        wide_block = block.astype(F32)
        rank = (
            wide_block[:, features : features + 1] * RADIX
            + wide_block[:, features + 1 : features + 2]
        )
        level = (2.0 * rank + 1.0) / float(total) - 1.0
        found = embed(block[:, :features], spread, column_bin, table[...])
        found = found + level * rank_vector[...].astype(F32)
        hist_rows[at, :] = found
        normed = normalize(found).astype(BF16)
        hist_normed[at, :] = normed
        keys_out[index] = dot(normed, w_key[...]).T.astype(BF16)
        values_out[index] = dot(normed, w_value[...]).astype(BF16)
        return carry

    lax.fori_loop(0, total // hist_tile, hist_step, 0)
    at = pl.ds(pl.multiple_of(me * own, own), own)
    rows_out[query_count:, :] = hist_rows[at, :]
    queries_out[query_count:, :] = dot(hist_normed[at, :], w_query[...]).astype(BF16)


def layer_kernel(
    sizes,
    rows,
    queries,
    keys,
    values,
    w_out,
    w_up,
    w_down,
    query_out,
    hist_out,
    key_pairs,
    value_pairs,
):
    own, ff_tile = sizes
    chunks, width, key_count = keys.shape
    head_dim = width // HEADS
    pairs = HEADS // 2
    tile = rows.shape[0]
    factor = math.log2(math.e) * head_dim ** (-0.5)

    @pl.when(pl.program_id(0) == 0)
    def _():
        left = lax.broadcasted_iota(jnp.int32, (key_count, LANES), 1) < head_dim
        upper = lax.broadcasted_iota(jnp.int32, (LANES, key_count), 0) < head_dim
        one = jnp.ones((key_count, LANES), F32)

        def arrange(chunk, carry):
            for pair in range(pairs):
                span = slice(pair * LANES, (pair + 1) * LANES)
                key = keys[chunk, span, :].astype(F32)
                key_pairs[chunk, pair, :, :key_count] = jnp.where(upper, key, 0.0).astype(BF16)
                key_pairs[chunk, pair, :, key_count:] = jnp.where(upper, 0.0, key).astype(BF16)
                value = values[chunk, :, span].astype(F32)
                for half, top in ((0, True), (1, False)):
                    at = slice(half * key_count, (half + 1) * key_count)
                    keep = left if top else jnp.logical_not(left)
                    value_pairs[chunk, pair, at, :LANES] = jnp.where(keep, value, 0.0).astype(BF16)
                    value_pairs[chunk, pair, at, LANES:] = jnp.where(keep, one, 0.0).astype(BF16)
            return carry

        lax.fori_loop(0, chunks, arrange, 0)

    def pair_scores(chunk, pair):
        scores = dot(queries[:, pair * LANES : (pair + 1) * LANES], key_pairs[chunk, pair])
        return scores[:, :key_count], scores[:, key_count:]

    def weigh(scores, peak):
        return jnp.exp2((scores - peak) * factor).astype(BF16)

    attended = []
    for pair in range(pairs):
        even, odd = pair_scores(0, pair)
        peaks = [jnp.max(even, axis=1, keepdims=True), jnp.max(odd, axis=1, keepdims=True)]
        weights = jnp.concatenate([weigh(even, peaks[0]), weigh(odd, peaks[1])], axis=1)
        summed = dot(weights, value_pairs[0, pair])
        if chunks > 1:

            def absorb(chunk, carry, pair=pair):
                peak_even, peak_odd, summed = carry
                even, odd = pair_scores(chunk, pair)
                new_even = jnp.maximum(peak_even, jnp.max(even, axis=1, keepdims=True))
                new_odd = jnp.maximum(peak_odd, jnp.max(odd, axis=1, keepdims=True))
                weights = jnp.concatenate([weigh(even, new_even), weigh(odd, new_odd)], axis=1)
                lane = lax.broadcasted_iota(jnp.int32, summed.shape, 1) % LANES
                fade = jnp.where(
                    lane < head_dim,
                    jnp.exp2((peak_even - new_even) * factor),
                    jnp.exp2((peak_odd - new_odd) * factor),
                )
                summed = summed * fade + dot(weights, value_pairs[chunk, pair])
                return (new_even, new_odd, summed)

            summed = lax.fori_loop(1, chunks, absorb, (peaks[0], peaks[1], summed))[2]
        attended.append((summed[:, :LANES] / summed[:, LANES:]).astype(BF16))
    after = rows[...] + dot(jnp.concatenate(attended, axis=1), w_out[...])
    normed = normalize(after).astype(BF16)
    result = after
    for start in range(0, w_up.shape[1], ff_tile):
        inner = dot(normed, w_up[:, start : start + ff_tile])
        hidden = jax.nn.gelu(inner, approximate=True).astype(BF16)
        result = result + dot(hidden, w_down[start : start + ff_tile, :])
    result = result.astype(BF16)
    query_out[...] = result

    @pl.when(pl.program_id(0) == pl.num_programs(0) - 1)
    def _():
        hist_out[...] = result[tile - own :, :]


def local(
    inner,
    count,
    hist_bins,
    hist_ranks,
    query_bins,
    bin_table,
    rank_vector,
    w_query,
    w_key,
    w_value,
    w_out,
    w_up,
    w_down,
):
    own = hist_bins.shape[0]
    query_count = query_bins.shape[0]
    width = bin_table.shape[1]
    total = own * count
    row_count = own + query_count
    hist_tile = math.gcd(total, 512)
    query_tile = math.gcd(query_count, 256)
    chunks = total // hist_tile
    vmem = pl.BlockSpec(memory_space=pltpu.VMEM)
    rows, queries, keys, values = pl.pallas_call(
        functools.partial(embed_kernel, (inner, count, query_tile, hist_tile)),
        out_shape=(
            jax.ShapeDtypeStruct((row_count, width), F32),
            jax.ShapeDtypeStruct((row_count, width), BF16),
            jax.ShapeDtypeStruct((chunks, width, hist_tile), BF16),
            jax.ShapeDtypeStruct((chunks, hist_tile, width), BF16),
        ),
        in_specs=[vmem] * 8,
        out_specs=(vmem,) * 4,
        scratch_shapes=[
            pltpu.VMEM((own, LANES), F32),
            pltpu.VMEM((own, LANES), BF16),
            pltpu.VMEM((count, own, LANES), BF16),
            pltpu.VMEM((total, width), F32),
            pltpu.VMEM((total, width), BF16),
            pltpu.SemaphoreType.DMA((count,)),
            pltpu.SemaphoreType.DMA((count,)),
        ],
        compiler_params=pltpu.CompilerParams(
            collective_id=0, has_side_effects=True, vmem_limit_bytes=40 << 20
        ),
        name="embed_rows",
    )(
        query_bins,
        hist_bins,
        hist_ranks.reshape(1, own),
        bin_table,
        rank_vector.reshape(1, width),
        w_query,
        w_key,
        w_value,
    )
    tile = max(
        size for size in range(16, 257, 16) if row_count % size == 0 and size >= own
    )

    def whole(shape):
        return pl.BlockSpec(
            shape, lambda i: (0,) * len(shape), pipeline_mode=pl.Buffered(1)
        )

    query_out, hist_out = pl.pallas_call(
        functools.partial(layer_kernel, (own, min(512, w_up.shape[1]))),
        out_shape=(
            jax.ShapeDtypeStruct((query_count, width), BF16),
            jax.ShapeDtypeStruct((own, width), BF16),
        ),
        grid=(row_count // tile,),
        in_specs=[
            pl.BlockSpec((tile, width), lambda i: (i, 0)),
            pl.BlockSpec((tile, width), lambda i: (i, 0)),
            whole(keys.shape),
            whole(values.shape),
            whole(w_out.shape),
            whole(w_up.shape),
            whole(w_down.shape),
        ],
        out_specs=(
            pl.BlockSpec((tile, width), lambda i: (i, 0)),
            pl.BlockSpec((own, width), lambda i: (0, 0)),
        ),
        scratch_shapes=[
            pltpu.VMEM((chunks, HEADS // 2, LANES, 2 * hist_tile), BF16),
            pltpu.VMEM((chunks, HEADS // 2, 2 * hist_tile, 2 * LANES), BF16),
        ],
        compiler_params=pltpu.CompilerParams(vmem_limit_bytes=56 << 20),
        name="layer_rows",
    )(rows, queries, keys, values, w_out, w_up, w_down)
    return (hist_out, query_out)


def solution(mesh):
    inner = mesh.shape["qry"]
    split = P(("ctx", "qry"), None)
    return jax.shard_map(
        functools.partial(local, inner, mesh.shape["ctx"] * inner),
        mesh=mesh,
        in_specs=(split, P(("ctx", "qry")), split) + (P(),) * 8,
        out_specs=(split, split),
        check_vma=False,
    )
```

time: 155 us -> 47.3 us (0.31); the launches traced: 153 us -> 46.9 us
  local copies, waits for them, and re-layouts: 53.6 us -> 11.3 us
  waiting for transfers between devices: 37 us -> 0 us
  Pallas kernels: 0 us -> 34.9 us
  matrix products: 28.3 us -> 0 us
  other arithmetic: 17.1 us -> 0 us
  blocking collectives: 15.2 us -> 0 us
    ppermute x7 -> x0, waiting for transfers between devices: 37 us -> none  [passed_along(): return lax.ppermute(block, axis, route)]
    pallas_call x0 -> x2, Pallas kernels: none -> 34.9 us  [the longest x1 21 us: local(): pl.pallas_call(functools.partial(layer_kernel, (own, min(512, w_up.shape[...]
    dot_general x23 -> x0, matrix products: 28.3 us -> none  [the longest x8 9.39 us: absorb_pair(): jnp.einsum('hnk,khd->hnd', weights.astype(jnp.bfloat16), value_heads, pre...]
    while x112 -> x0, local copies, waits for them, and re-layouts: 18.7 us -> none
    slice x19 -> x0, local copies, waits for them, and re-layouts: 16.8 us -> none  [the longest x15 12.1 us: absorb(): return absorb_pair(carry_state, arrived[0], arrived[1])]
    all_gather x1 -> x0, blocking collectives: 15.2 us -> none  [local(): first_block = lax.all_gather(key_pairs, 'qry', axis=1, tiled=True)]
    eq x16 -> x0, other arithmetic: 8.22 us -> none  [embed_bins(): bin_rows[:, feature:feature + 1] == columns]
    unnamed x26 -> x21, local copies, waits for them, and re-layouts: 2.72 us -> 10.6 us
  transfers between devices with their start and end apart: 7 -> 0, of which waited for: 7 -> 0; matrix products, arithmetic and copies ran while one was open for 0% -> 0% of each run, Pallas kernels for 0% -> 0%
where the time goes in v1:
time: 47.3 us; the launch traced here: 46.9 us
  Pallas kernels  34.9 us (74%)
  local copies, waits for them, and re-layouts  11.3 us (24%)
  between operations  0.67 us (1%)
    pallas_call x1, Pallas kernels, local(): pl.pallas_call(functools.partial(layer_kernel, (own, min(512, w_up.shape[...  21 us
    pallas_call x1, Pallas kernels, local(): pl.pallas_call(functools.partial(embed_kernel, (inner, count, query_tile,...  14 us
    unnamed x21, local copies, waits for them, and re-layouts  10.6 us

profile of v1, /device:TPU:0, one launch (start us, length us, event | category | flops | bytes accessed | tf_op | source)
XLA Modules:
  0.0 46.9 jit_solution(15882642338837431441)
XLA Ops:
  0.6 0.7 %reshape.11.rank_vector = bf16[1,512]{1,0:T(2,128)(2,1)S(1)} reshape(bf16[512]{0:T(512)(128)(2,1)} %param.15) | data formatting | bytes 2048 | tf_op jit(solution)/shard_map/reshape | solution.py:319
  1.3 1.0 %copy.13.query_bins = s32[1024,16]{1,0:T(8,128)S(1)} copy(s32[1024,16]{0,1:T(8,128)} %param.13) | data formatting | bytes 131072 | tf_op args[2]
  2.4 0.0 copy-start.2
  2.4 1.2 %copy-done.2 = bf16[1024,512]{1,0:T(8,128)(2,1)S(1)} copy-done((bf16[1024,512]{1,0:T(8,128)(2,1)S(1)}, bf16[1024,512]{1,0:T(8,128)(2,1)}, u32[]{:S(2)}) %copy-start.2) | copy-done | bytes 1048600
  3.6 0.0 copy-start.5
  3.6 1.0 %copy-done.5 = bf16[512,512]{1,0:T(8,128)(2,1)S(1)} copy-done((bf16[512,512]{1,0:T(8,128)(2,1)S(1)}, bf16[512,512]{1,0:T(8,128)(2,1)}, u32[]{:S(2)}) %copy-start.5) | copy-done | bytes 524312
  4.6 0.0 copy-start.6
  4.6 1.0 %copy-done.6 = bf16[512,512]{1,0:T(8,128)(2,1)S(1)} copy-done((bf16[512,512]{1,0:T(8,128)(2,1)S(1)}, bf16[512,512]{1,0:T(8,128)(2,1)}, u32[]{:S(2)}) %copy-start.6) | copy-done | bytes 524312
  5.7 0.0 copy-start.7
  5.7 1.0 %copy-done.7 = bf16[512,512]{1,0:T(8,128)(2,1)S(1)} copy-done((bf16[512,512]{1,0:T(8,128)(2,1)S(1)}, bf16[512,512]{1,0:T(8,128)(2,1)}, u32[]{:S(2)}) %copy-start.7) | copy-done | bytes 524312
  6.7 0.0 copy-start.8
  6.7 0.7 %copy-done.8 = s32[16,16]{1,0:T(8,128)S(1)} copy-done((s32[16,16]{1,0:T(8,128)S(1)}, s32[16,16]{1,0:T(8,128)}, u32[]{:S(2)}) %copy-start.8) | copy-done | bytes 1048
  7.4 0.0 copy-start.9
  7.4 0.7 %copy-done.9 = s32[16]{0:T(128)S(1)} copy-done((s32[16]{0:T(128)S(1)}, s32[16]{0:T(128)}, u32[]{:S(2)}) %copy-start.9) | copy-done | bytes 88
  8.1 14.0 %embed_rows.1 = (f32[1040,512]{1,0:T(8,128)S(1)}, bf16[1040,512]{1,0:T(8,128)(2,1)S(1)}, bf16[1,512,512]{2,1,0:T(8,128)(2,1)S(1)}, bf16[1,512,512]{2,1,0:T(8,128)(2,1)S(1)}) custom-call(s32[1024,16]{1,0:T(8,128)S(1)} %copy.13.query_bins, s32[16,16]{1,0:T(8,128)S(1)} %copy-done.8, s32[1,16]{1,0:T(1,128)S(1)} %bitcast.1, bf16[1024,512]{1,0:T(8,128)(2,1)S(1)} %copy-done.2, ...), custom_call_target="tpu_custom_call" | custom-call | tf_op jit(solution)/shard_map/embed_rows/pallas_call | solution.py:291
  22.0 0.0 copy-start
  22.0 1.3 %copy-done = f32[1040,512]{1,0:T(8,128)} copy-done((f32[1040,512]{1,0:T(8,128)}, f32[1040,512]{1,0:T(8,128)S(1)}, u32[]{:S(2)}) %copy-start) | copy-done | bytes 2129944
  23.4 0.0 copy-start.1
  23.4 1.0 %copy-done.1 = bf16[1040,512]{1,0:T(8,128)(2,1)} copy-done((bf16[1040,512]{1,0:T(8,128)(2,1)}, bf16[1040,512]{1,0:T(8,128)(2,1)S(1)}, u32[]{:S(2)}) %copy-start.1) | copy-done | bytes 1064984
  24.3 0.0 copy-start.3
  24.3 0.8 %copy-done.3 = bf16[1,512,512]{2,1,0:T(8,128)(2,1)} copy-done((bf16[1,512,512]{2,1,0:T(8,128)(2,1)}, bf16[1,512,512]{2,1,0:T(8,128)(2,1)S(1)}, u32[]{:S(2)}) %copy-start.3) | copy-done | bytes 524312
  25.1 0.0 copy-start.4
  25.2 0.8 %copy-done.4 = bf16[1,512,512]{2,1,0:T(8,128)(2,1)} copy-done((bf16[1,512,512]{2,1,0:T(8,128)(2,1)}, bf16[1,512,512]{2,1,0:T(8,128)(2,1)S(1)}, u32[]{:S(2)}) %copy-start.4) | copy-done | bytes 524312
  25.9 21.0 %layer_rows.1 = (bf16[1024,512]{1,0:T(8,128)(2,1)}, bf16[16,512]{1,0:T(8,128)(2,1)}) custom-call(f32[1040,512]{1,0:T(8,128)} %copy-done, bf16[1040,512]{1,0:T(8,128)(2,1)} %copy-done.1, bf16[1,512,512]{2,1,0:T(8,128)(2,1)} %copy-done.3, bf16[1,512,512]{2,1,0:T(8,128)(2,1)} %copy-done.4, bf16[512,512]{1,0:T(8,128)(2,1)} %w_out.1, bf16[512,2048]{1,0:T(8,128)(2,1)} %w_up.1, ...), custom_call_target="tpu_custom_call" | custom-call | tf_op jit(solution)/shard_map/layer_rows/pallas_call | solution.py:333
Async XLA Ops:
  2.4 1.2 %copy-start.2 = (bf16[1024,512]{1,0:T(8,128)(2,1)S(1)}, bf16[1024,512]{1,0:T(8,128)(2,1)}, u32[]{:S(2)}) copy-start(bf16[1024,512]{1,0:T(8,128)(2,1)} %table.1) | copy-start | bytes 3145732
  3.6 1.0 %copy-start.5 = (bf16[512,512]{1,0:T(8,128)(2,1)S(1)}, bf16[512,512]{1,0:T(8,128)(2,1)}, u32[]{:S(2)}) copy-start(bf16[512,512]{1,0:T(8,128)(2,1)} %w_query.1) | copy-start | bytes 1572868
  4.6 1.0 %copy-start.6 = (bf16[512,512]{1,0:T(8,128)(2,1)S(1)}, bf16[512,512]{1,0:T(8,128)(2,1)}, u32[]{:S(2)}) copy-start(bf16[512,512]{1,0:T(8,128)(2,1)} %w_key.1) | copy-start | bytes 1572868
  5.7 1.0 %copy-start.7 = (bf16[512,512]{1,0:T(8,128)(2,1)S(1)}, bf16[512,512]{1,0:T(8,128)(2,1)}, u32[]{:S(2)}) copy-start(bf16[512,512]{1,0:T(8,128)(2,1)} %w_value.1) | copy-start | bytes 1572868
  6.7 0.7 %copy-start.8 = (s32[16,16]{1,0:T(8,128)S(1)}, s32[16,16]{1,0:T(8,128)}, u32[]{:S(2)}) copy-start(s32[16,16]{1,0:T(8,128)} %hist_bins.1) | copy-start | bytes 3076
  7.4 0.7 %copy-start.9 = (s32[16]{0:T(128)S(1)}, s32[16]{0:T(128)}, u32[]{:S(2)}) copy-start(s32[16]{0:T(128)} %param.12) | copy-start | bytes 196
  22.0 1.3 %copy-start = (f32[1040,512]{1,0:T(8,128)}, f32[1040,512]{1,0:T(8,128)S(1)}, u32[]{:S(2)}) copy-start(f32[1040,512]{1,0:T(8,128)S(1)} %get-tuple-element.8.rows) | copy-start | bytes 6389764
  23.4 1.0 %copy-start.1 = (bf16[1040,512]{1,0:T(8,128)(2,1)}, bf16[1040,512]{1,0:T(8,128)(2,1)S(1)}, u32[]{:S(2)}) copy-start(bf16[1040,512]{1,0:T(8,128)(2,1)S(1)} %get-tuple-element.9.queries) | copy-start | bytes 3194884
  24.3 0.8 %copy-start.3 = (bf16[1,512,512]{2,1,0:T(8,128)(2,1)}, bf16[1,512,512]{2,1,0:T(8,128)(2,1)S(1)}, u32[]{:S(2)}) copy-start(bf16[1,512,512]{2,1,0:T(8,128)(2,1)S(1)} %get-tuple-element.10.keys) | copy-start | bytes 1572868
  25.1 0.8 %copy-start.4 = (bf16[1,512,512]{2,1,0:T(8,128)(2,1)}, bf16[1,512,512]{2,1,0:T(8,128)(2,1)S(1)}, u32[]{:S(2)}) copy-start(bf16[1,512,512]{2,1,0:T(8,128)(2,1)S(1)} %get-tuple-element.11.values) | copy-start | bytes 1572868

commit v2 on v1

v2 whole, which is shorter than its diff:
```python
import functools
import math

import jax
import jax.numpy as jnp
from jax import lax
from jax.experimental import pallas as pl
from jax.experimental.pallas import tpu as pltpu
from jax.sharding import PartitionSpec as P

HEADS = 8
LANES = 128
RADIX = 64
VMEM_LIMIT = 64 << 20
epsilon = 1e-05
F32 = jnp.float32
BF16 = jnp.bfloat16


def normalize(values):
    centered = values - jnp.mean(values, axis=-1, keepdims=True)
    variance = jnp.mean(centered * centered, axis=-1, keepdims=True)
    return centered * lax.rsqrt(variance + epsilon)


def dot(a, b):
    return jnp.dot(a, b, preferred_element_type=F32)


def embed(named, column_bin, table):
    one_hot = jnp.where(named == column_bin, 1.0, 0.0).astype(BF16)
    return dot(one_hot, table)


def layer_kernel(
    sizes,
    query_bins_hbm,
    hist_bins_hbm,
    hist_ranks_hbm,
    table_hbm,
    rank_vector_hbm,
    w_query_hbm,
    w_key_hbm,
    w_value_hbm,
    w_out_hbm,
    w_up_hbm,
    w_down_hbm,
    hist_out,
    query_out,
    query_bins,
    hist_bins,
    hist_ranks,
    table,
    rank_vector,
    w_query,
    w_key,
    w_value,
    w_out,
    w_up,
    w_down,
    fetch_sem,
    store_sem,
    rows_out,
    queries_out,
    results,
    key_pairs,
    value_pairs,
    staged,
    mine,
    blocks,
    hist_rows,
    hist_normed,
    send_sem,
    recv_sem,
):
    inner, count, query_tile, hist_tile, tile, ff_tile = sizes
    own, features = hist_bins.shape
    query_count = query_bins.shape[1]
    total = count * own
    fetches = [
        pltpu.make_async_copy(source, target, fetch_sem.at[index])
        for index, (source, target) in enumerate(
            (
                (hist_bins_hbm, hist_bins),
                (hist_ranks_hbm, hist_ranks),
                (query_bins_hbm, query_bins),
                (table_hbm, table),
                (w_query_hbm, w_query),
                (rank_vector_hbm, rank_vector),
                (w_key_hbm, w_key),
                (w_value_hbm, w_value),
                (w_out_hbm, w_out),
                (w_up_hbm, w_up),
                (w_down_hbm, w_down),
            )
        )
    ]
    for fetch in fetches:
        fetch.start()
    me = lax.axis_index("ctx") * inner + lax.axis_index("qry")

    def place(index):
        return {"ctx": index // inner, "qry": index % inner}

    def partner(step):
        return (me + step) % count

    barrier = pltpu.get_barrier_semaphore()

    def greet(step, carry):
        pl.semaphore_signal(
            barrier,
            inc=1,
            device_id=place(partner(step)),
            device_id_type=pl.DeviceIdType.MESH,
        )
        return carry

    lax.fori_loop(1, count, greet, 0)

    fetches[0].wait()
    fetches[1].wait()
    ranks = jnp.broadcast_to(hist_ranks[...], (own, own))
    diagonal = lax.broadcasted_iota(jnp.int32, (own, own), 0) == lax.broadcasted_iota(
        jnp.int32, (own, own), 1
    )
    rank = jnp.sum(jnp.where(diagonal, ranks.astype(F32), 0.0), axis=1, keepdims=True)
    high = jnp.floor(rank * (1.0 / RADIX))
    staged[...] = jnp.zeros_like(staged)
    staged[:, :features] = hist_bins[...].astype(F32)
    staged[:, features : features + 1] = high
    staged[:, features + 1 : features + 2] = rank - high * RADIX
    mine[...] = staged[...].astype(BF16)
    blocks[me] = mine[...]

    bin_count = table.shape[0] // features
    wide = (features, table.shape[0])
    spread = jnp.where(
        lax.broadcasted_iota(jnp.int32, wide, 1) // bin_count
        == lax.broadcasted_iota(jnp.int32, wide, 0),
        1.0,
        0.0,
    ).astype(BF16)
    column_bin = (
        lax.broadcasted_iota(jnp.int32, (1, table.shape[0]), 1) % bin_count
    ).astype(F32)

    def copy_to(step):
        other = partner(step)
        return pltpu.make_async_remote_copy(
            src_ref=mine,
            dst_ref=blocks.at[me],
            send_sem=send_sem.at[other],
            recv_sem=recv_sem.at[me],
            device_id=place(other),
            device_id_type=pl.DeviceIdType.MESH,
        )

    def copy_from(step):
        other = partner(step)
        return pltpu.make_async_remote_copy(
            src_ref=mine,
            dst_ref=blocks.at[other],
            send_sem=send_sem.at[other],
            recv_sem=recv_sem.at[other],
            device_id=place(other),
            device_id_type=pl.DeviceIdType.MESH,
        )

    def send(step, carry):
        copy_to(step).start()
        return carry

    pl.semaphore_wait(barrier, count - 1)
    lax.fori_loop(1, count, send, 0)

    for fetch in fetches[2:5]:
        fetch.wait()

    def query_step(index, carry):
        at = pl.ds(pl.multiple_of(index * query_tile, query_tile), query_tile)
        named = lax.dot_general(
            query_bins[:, at].astype(F32).astype(BF16),
            spread,
            (((0,), (0,)), ((), ())),
            preferred_element_type=F32,
        )
        found = embed(named, column_bin, table[...])
        rows_out[at, :] = found
        queries_out[at, :] = dot(normalize(found).astype(BF16), w_query[...]).astype(BF16)
        return carry

    lax.fori_loop(0, query_count // query_tile, query_step, 0)

    def finish(step, carry):
        copy_to(step).wait_send()
        copy_from(step).wait_recv()
        return carry

    for fetch in fetches[5:8]:
        fetch.wait()
    lax.fori_loop(1, count, finish, 0)

    width = table.shape[1]
    head_dim = width // HEADS
    pairs = HEADS // 2
    left = lax.broadcasted_iota(jnp.int32, (hist_tile, LANES), 1) < head_dim
    upper = lax.broadcasted_iota(jnp.int32, (LANES, hist_tile), 0) < head_dim

    def hist_step(index, carry):
        tile_blocks = hist_tile // own
        block = blocks[pl.ds(index * tile_blocks, tile_blocks)].reshape(hist_tile, LANES)
        at = pl.ds(pl.multiple_of(index * hist_tile, hist_tile), hist_tile)
        wide_block = block.astype(F32)
        rank = (
            wide_block[:, features : features + 1] * RADIX
            + wide_block[:, features + 1 : features + 2]
        )
        level = (2.0 * rank + 1.0) / float(total) - 1.0
        found = embed(dot(block[:, :features], spread), column_bin, table[...])
        found = found + level * rank_vector[...].astype(F32).reshape(1, -1)
        hist_rows[at, :] = found
        normed = normalize(found).astype(BF16)
        hist_normed[at, :] = normed
        keys = dot(normed, w_key[...]).T
        values = dot(normed, w_value[...])
        for pair in range(pairs):
            span = slice(pair * LANES, (pair + 1) * LANES)
            key = keys[span, :]
            key_pairs[index, pair, :, :hist_tile] = jnp.where(upper, key, 0.0).astype(BF16)
            key_pairs[index, pair, :, hist_tile:] = jnp.where(upper, 0.0, key).astype(BF16)
            value = values[:, span]
            for half, keep in ((0, left), (1, jnp.logical_not(left))):
                part = slice(half * hist_tile, (half + 1) * hist_tile)
                value_pairs[index, pair, part, :LANES] = jnp.where(keep, value, 0.0).astype(BF16)
                value_pairs[index, pair, part, LANES:] = jnp.where(keep, 1.0, 0.0).astype(BF16)
        return carry

    lax.fori_loop(0, total // hist_tile, hist_step, 0)
    at = pl.ds(pl.multiple_of(me * own, own), own)
    rows_out[query_count:, :] = hist_rows[at, :]
    queries_out[query_count:, :] = dot(hist_normed[at, :], w_query[...]).astype(BF16)

    factor = math.log2(math.e) * head_dim ** (-0.5)
    chunks = total // hist_tile
    tiles = (query_count + own) // tile
    for fetch in fetches[8:]:
        fetch.wait()

    def store(index):
        at = pl.ds(pl.multiple_of(index * tile, tile), tile)
        return pltpu.make_async_copy(results.at[at], query_out.at[at], store_sem.at[index])

    def pair_scores(at, chunk, pair):
        scores = dot(queries_out[at, pair * LANES : (pair + 1) * LANES], key_pairs[chunk, pair])
        return scores[:, :hist_tile], scores[:, hist_tile:]

    def weigh(scores, peak):
        return jnp.exp2((scores - peak) * factor).astype(BF16)

    def tile_step(index, carry):
        at = pl.ds(pl.multiple_of(index * tile, tile), tile)
        attended = []
        for pair in range(pairs):
            even, odd = pair_scores(at, 0, pair)
            peaks = [jnp.max(even, axis=1, keepdims=True), jnp.max(odd, axis=1, keepdims=True)]
            weights = jnp.concatenate([weigh(even, peaks[0]), weigh(odd, peaks[1])], axis=1)
            summed = dot(weights, value_pairs[0, pair])
            if chunks > 1:

                def absorb(chunk, carry, pair=pair):
                    peak_even, peak_odd, summed = carry
                    even, odd = pair_scores(at, chunk, pair)
                    new_even = jnp.maximum(peak_even, jnp.max(even, axis=1, keepdims=True))
                    new_odd = jnp.maximum(peak_odd, jnp.max(odd, axis=1, keepdims=True))
                    weights = jnp.concatenate([weigh(even, new_even), weigh(odd, new_odd)], axis=1)
                    lane = lax.broadcasted_iota(jnp.int32, summed.shape, 1) % LANES
                    fade = jnp.where(
                        lane < head_dim,
                        jnp.exp2((peak_even - new_even) * factor),
                        jnp.exp2((peak_odd - new_odd) * factor),
                    )
                    summed = summed * fade + dot(weights, value_pairs[chunk, pair])
                    return (new_even, new_odd, summed)

                summed = lax.fori_loop(1, chunks, absorb, (peaks[0], peaks[1], summed))[2]
            attended.append((summed[:, :LANES] / summed[:, LANES:]).astype(BF16))

        after = rows_out[at, :] + dot(jnp.concatenate(attended, axis=1), w_out[...])
        normed = normalize(after).astype(BF16)
        result = after
        for start in range(0, w_up.shape[1], ff_tile):
            inner = dot(normed, w_up[:, start : start + ff_tile])
            hidden = jax.nn.gelu(inner, approximate=True).astype(BF16)
            result = result + dot(hidden, w_down[start : start + ff_tile, :])
        results[at, :] = result.astype(BF16)

        @pl.when(index < tiles - 1)
        def _():
            store(index).start()

        return carry

    lax.fori_loop(0, tiles, tile_step, 0)
    last = slice((tiles - 1) * tile, query_count)
    ending = [
        pltpu.make_async_copy(results.at[last], query_out.at[last], store_sem.at[tiles - 1]),
        pltpu.make_async_copy(results.at[query_count:], hist_out, store_sem.at[tiles]),
    ]
    for part in ending:
        part.start()
    for index in range(tiles - 1):
        store(index).wait()
    for part in ending:
        part.wait()


def local(
    inner,
    count,
    hist_bins,
    hist_ranks,
    query_bins,
    bin_table,
    rank_vector,
    w_query,
    w_key,
    w_value,
    w_out,
    w_up,
    w_down,
):
    own = hist_bins.shape[0]
    query_count = query_bins.shape[0]
    width = bin_table.shape[1]
    total = own * count
    row_count = own + query_count
    hist_tile = math.gcd(total, 512)
    query_tile = math.gcd(query_count, 256)
    chunks = total // hist_tile
    features = hist_bins.shape[1]
    pairs = HEADS // 2
    tile = max(
        size for size in range(16, 257, 16) if row_count % size == 0 and size > own
    )
    tiles = row_count // tile
    hbm = pl.BlockSpec(memory_space=pltpu.HBM)
    return pl.pallas_call(
        functools.partial(
            layer_kernel,
            (inner, count, query_tile, hist_tile, tile, min(512, w_up.shape[1])),
        ),
        out_shape=(
            jax.ShapeDtypeStruct((own, width), BF16),
            jax.ShapeDtypeStruct((query_count, width), BF16),
        ),
        in_specs=[hbm] * 11,
        out_specs=(hbm, hbm),
        scratch_shapes=[
            pltpu.VMEM((features, query_count), jnp.int32),
            pltpu.VMEM((own, features), jnp.int32),
            pltpu.VMEM((1, own), jnp.int32),
            pltpu.VMEM(bin_table.shape, BF16),
            pltpu.VMEM(rank_vector.shape, BF16),
            pltpu.VMEM(w_query.shape, BF16),
            pltpu.VMEM(w_key.shape, BF16),
            pltpu.VMEM(w_value.shape, BF16),
            pltpu.VMEM(w_out.shape, BF16),
            pltpu.VMEM(w_up.shape, BF16),
            pltpu.VMEM(w_down.shape, BF16),
            pltpu.SemaphoreType.DMA((11,)),
            pltpu.SemaphoreType.DMA((tiles + 1,)),
            pltpu.VMEM((row_count, width), F32),
            pltpu.VMEM((row_count, width), BF16),
            pltpu.VMEM((row_count, width), BF16),
            pltpu.VMEM((chunks, pairs, LANES, 2 * hist_tile), BF16),
            pltpu.VMEM((chunks, pairs, 2 * hist_tile, 2 * LANES), BF16),
            pltpu.VMEM((own, LANES), F32),
            pltpu.VMEM((own, LANES), BF16),
            pltpu.VMEM((count, own, LANES), BF16),
            pltpu.VMEM((total, width), F32),
            pltpu.VMEM((total, width), BF16),
            pltpu.SemaphoreType.DMA((count,)),
            pltpu.SemaphoreType.DMA((count,)),
        ],
        compiler_params=pltpu.CompilerParams(
            collective_id=0, has_side_effects=True, vmem_limit_bytes=VMEM_LIMIT
        ),
        name="layer_rows",
    )(
        query_bins.T,
        hist_bins,
        hist_ranks.reshape(1, own),
        bin_table,
        rank_vector,
        w_query,
        w_key,
        w_value,
        w_out,
        w_up,
        w_down,
    )


def solution(mesh):
    inner = mesh.shape["qry"]
    split = P(("ctx", "qry"), None)
    return jax.shard_map(
        functools.partial(local, inner, mesh.shape["ctx"] * inner),
        mesh=mesh,
        in_specs=(split, P(("ctx", "qry")), split) + (P(),) * 8,
        out_specs=(split, split),
        check_vma=False,
    )
```

time: 47.3 us -> 36.5 us (0.77)
  local copies, waits for them, and re-layouts: 11.3 us -> 3.59 us
  Pallas kernels: 34.9 us -> 32 us
    unnamed x21 -> x2, local copies, waits for them, and re-layouts: 10.6 us -> 3.59 us
    pallas_call x2 -> x1, Pallas kernels: 34.9 us -> 32 us  [local(): pl.pallas_call(functools.partial(layer_kernel, (inner, count, query_tile,...]
    reshape x1 -> x0, local copies, waits for them, and re-layouts: 0.68 us -> none  [local(): rank_vector.reshape(1, width)]
where the time goes in v2:
time: 36.5 us; the launch traced here: 36.2 us
  Pallas kernels  32 us (88%)
  local copies, waits for them, and re-layouts  3.59 us (10%)
  between operations  0.64 us (2%)
    pallas_call x1, Pallas kernels, local(): pl.pallas_call(functools.partial(layer_kernel, (inner, count, query_tile,...  32 us
    unnamed x2, local copies, waits for them, and re-layouts  3.59 us

profile of v2, /device:TPU:0, one launch (start us, length us, event | category | flops | bytes accessed | tf_op | source)
XLA Modules:
  0.0 36.2 jit_solution(5949970729951622926)
XLA Ops:
  0.6 32.0 %layer_rows.1 = (bf16[16,512]{1,0:T(8,128)(2,1)}, bf16[1024,512]{1,0:T(8,128)(2,1)}) custom-call(s32[16,1024]{1,0:T(8,128)} %bitcast.2, s32[16,16]{1,0:T(8,128)} %hist_bins_hbm.1, s32[1,16]{1,0:T(1,128)} %bitcast.3, bf16[1024,512]{1,0:T(8,128)(2,1)} %table_hbm.1, bf16[512]{0:T(512)(128)(2,1)} %rank_vector_hbm.1, bf16[512,512]{1,0:T(8,128)(2,1)} %w_query_hbm.1, ...), custom_call_target="tpu_custom_call" | custom-call | tf_op jit(solution)/shard_map/layer_rows/pallas_call | solution.py:348
  32.6 1.3 %copy.15 = bf16[16,512]{1,0:T(8,128)(2,1)} copy(bf16[16,512]{1,0:T(8,128)(2,1)} %get-tuple-element.4) | data formatting | bytes 32768
  34.0 2.3 %copy.16 = bf16[1024,512]{1,0:T(8,128)(2,1)} copy(bf16[1024,512]{1,0:T(8,128)(2,1)} %get-tuple-element.5) | data formatting | bytes 2097152

commit v3 on v2

--- a/solution.py
+++ b/solution.py
@@ -60,9 +60,9 @@
     w_down,
     fetch_sem,
     store_sem,
+    results,
     rows_out,
     queries_out,
-    results,
     key_pairs,
     value_pairs,
     staged,
@@ -73,7 +73,7 @@
     send_sem,
     recv_sem,
 ):
-    inner, count, query_tile, hist_tile, tile, ff_tile = sizes
+    inner, count, query_tile, hist_tile, tile = sizes
     own, features = hist_bins.shape
     query_count = query_bins.shape[1]
     total = count * own
@@ -190,7 +190,7 @@
         queries_out[at, :] = dot(normalize(found).astype(BF16), w_query[...]).astype(BF16)
         return carry
 
-    lax.fori_loop(0, query_count // query_tile, query_step, 0)
+    lax.fori_loop(0, query_count // query_tile, query_step, 0, unroll=True)
 
     def finish(step, carry):
         copy_to(step).wait_send()
@@ -247,10 +247,6 @@
     for fetch in fetches[8:]:
         fetch.wait()
 
-    def store(index):
-        at = pl.ds(pl.multiple_of(index * tile, tile), tile)
-        return pltpu.make_async_copy(results.at[at], query_out.at[at], store_sem.at[index])
-
     def pair_scores(at, chunk, pair):
         scores = dot(queries_out[at, pair * LANES : (pair + 1) * LANES], key_pairs[chunk, pair])
         return scores[:, :hist_tile], scores[:, hist_tile:]
@@ -258,51 +254,76 @@
     def weigh(scores, peak):
         return jnp.exp2((scores - peak) * factor).astype(BF16)
 
+    def attend(at, pair):
+        even, odd = pair_scores(at, 0, pair)
+        peaks = [jnp.max(even, axis=1, keepdims=True), jnp.max(odd, axis=1, keepdims=True)]
+        weights = jnp.concatenate([weigh(even, peaks[0]), weigh(odd, peaks[1])], axis=1)
+        summed = dot(weights, value_pairs[0, pair])
+        if chunks > 1:
+
+            def absorb(chunk, carry):
+                peak_even, peak_odd, summed = carry
+                even, odd = pair_scores(at, chunk, pair)
+                new_even = jnp.maximum(peak_even, jnp.max(even, axis=1, keepdims=True))
+                new_odd = jnp.maximum(peak_odd, jnp.max(odd, axis=1, keepdims=True))
+                weights = jnp.concatenate([weigh(even, new_even), weigh(odd, new_odd)], axis=1)
+                lane = lax.broadcasted_iota(jnp.int32, summed.shape, 1) % LANES
+                fade = jnp.where(
+                    lane < head_dim,
+                    jnp.exp2((peak_even - new_even) * factor),
+                    jnp.exp2((peak_odd - new_odd) * factor),
+                )
+                summed = summed * fade + dot(weights, value_pairs[chunk, pair])
+                return (new_even, new_odd, summed)
+
+            summed = lax.fori_loop(1, chunks, absorb, (peaks[0], peaks[1], summed))[2]
+        return (summed[:, :LANES] / summed[:, LANES:]).astype(BF16)
+
+    def project(at, attended):
+        after = rows_out[at, :] + dot(jnp.concatenate(attended, axis=1), w_out[...])
+        rows_out[at, :] = after
+        queries_out[at, :] = normalize(after).astype(BF16)
+
+    ff_tile = w_up.shape[1] // pairs
+
+    def feed(normed, part):
+        span = slice(part * ff_tile, (part + 1) * ff_tile)
+        hidden = jax.nn.gelu(dot(normed, w_up[:, span]), approximate=True).astype(BF16)
+        return dot(hidden, w_down[span, :])
+
+    def rows_at(index):
+        return pl.ds(pl.multiple_of(index * tile, tile), tile)
+
+    def store(index):
+        at = rows_at(index)
+        return pltpu.make_async_copy(results.at[at], query_out.at[at], store_sem.at[index])
+
+    first = slice(0, tile)
+    project(first, [attend(first, pair) for pair in range(pairs)])
+
     def tile_step(index, carry):
-        at = pl.ds(pl.multiple_of(index * tile, tile), tile)
+        at, before = rows_at(index), rows_at(index - 1)
+        normed = queries_out[before, :]
+        result = rows_out[before, :]
         attended = []
         for pair in range(pairs):
-            even, odd = pair_scores(at, 0, pair)
-            peaks = [jnp.max(even, axis=1, keepdims=True), jnp.max(odd, axis=1, keepdims=True)]
-            weights = jnp.concatenate([weigh(even, peaks[0]), weigh(odd, peaks[1])], axis=1)
-            summed = dot(weights, value_pairs[0, pair])
-            if chunks > 1:
-
-                def absorb(chunk, carry, pair=pair):
-                    peak_even, peak_odd, summed = carry
-                    even, odd = pair_scores(at, chunk, pair)
-                    new_even = jnp.maximum(peak_even, jnp.max(even, axis=1, keepdims=True))
-                    new_odd = jnp.maximum(peak_odd, jnp.max(odd, axis=1, keepdims=True))
-                    weights = jnp.concatenate([weigh(even, new_even), weigh(odd, new_odd)], axis=1)
-                    lane = lax.broadcasted_iota(jnp.int32, summed.shape, 1) % LANES
-                    fade = jnp.where(
-                        lane < head_dim,
-                        jnp.exp2((peak_even - new_even) * factor),
-                        jnp.exp2((peak_odd - new_odd) * factor),
-                    )
-                    summed = summed * fade + dot(weights, value_pairs[chunk, pair])
-                    return (new_even, new_odd, summed)
-
-                summed = lax.fori_loop(1, chunks, absorb, (peaks[0], peaks[1], summed))[2]
-            attended.append((summed[:, :LANES] / summed[:, LANES:]).astype(BF16))
-
-        after = rows_out[at, :] + dot(jnp.concatenate(attended, axis=1), w_out[...])
-        normed = normalize(after).astype(BF16)
-        result = after
-        for start in range(0, w_up.shape[1], ff_tile):
-            inner = dot(normed, w_up[:, start : start + ff_tile])
-            hidden = jax.nn.gelu(inner, approximate=True).astype(BF16)
-            result = result + dot(hidden, w_down[start : start + ff_tile, :])
-        results[at, :] = result.astype(BF16)
-
-        @pl.when(index < tiles - 1)
-        def _():
-            store(index).start()
-
-        return carry
-
-    lax.fori_loop(0, tiles, tile_step, 0)
-    last = slice((tiles - 1) * tile, query_count)
+            attended.append(attend(at, pair))
+            if pair < pairs - 1:
+                result = result + feed(normed, pair)
+        project(at, attended)
+        results[before, :] = (result + feed(normed, pairs - 1)).astype(BF16)
+        store(index - 1).start()
+        return carry
+
+    lax.fori_loop(1, tiles, tile_step, 0)
+    start = (tiles - 1) * tile
+    normed = queries_out[start:, :]
+    result = rows_out[start:, :]
+    for part in range(pairs):
+        result = result + feed(normed, part)
+    result = result.astype(BF16)
+    results[start:, :] = result
+    last = slice(start, query_count)
     ending = [
         pltpu.make_async_copy(results.at[last], query_out.at[last], store_sem.at[tiles - 1]),
         pltpu.make_async_copy(results.at[query_count:], hist_out, store_sem.at[tiles]),
@@ -343,12 +364,11 @@
     tile = max(
         size for size in range(16, 257, 16) if row_count % size == 0 and size > own
     )
-    tiles = row_count // tile
     hbm = pl.BlockSpec(memory_space=pltpu.HBM)
     return pl.pallas_call(
         functools.partial(
             layer_kernel,
-            (inner, count, query_tile, hist_tile, tile, min(512, w_up.shape[1])),
+            (inner, count, query_tile, hist_tile, tile),
         ),
         out_shape=(
             jax.ShapeDtypeStruct((own, width), BF16),
@@ -369,9 +389,9 @@
             pltpu.VMEM(w_up.shape, BF16),
             pltpu.VMEM(w_down.shape, BF16),
             pltpu.SemaphoreType.DMA((11,)),
-            pltpu.SemaphoreType.DMA((tiles + 1,)),
+            pltpu.SemaphoreType.DMA((row_count // tile + 1,)),
+            pltpu.VMEM((row_count, width), BF16),
             pltpu.VMEM((row_count, width), F32),
-            pltpu.VMEM((row_count, width), BF16),
             pltpu.VMEM((row_count, width), BF16),
             pltpu.VMEM((chunks, pairs, LANES, 2 * hist_tile), BF16),
             pltpu.VMEM((chunks, pairs, 2 * hist_tile, 2 * LANES), BF16),

time: 36.5 us -> 34.9 us (0.956)
  Pallas kernels: 32 us -> 30.4 us
    pallas_call x1, Pallas kernels: 32 us -> 30.4 us  [local(): pl.pallas_call(functools.partial(layer_kernel, (inner, count, query_tile,...]
where the time goes in v3:
time: 34.9 us; the launch traced here: 34.6 us
  Pallas kernels  30.4 us (87%)
  local copies, waits for them, and re-layouts  3.59 us (10%)
  between operations  0.64 us (2%)
    pallas_call x1, Pallas kernels, local(): pl.pallas_call(functools.partial(layer_kernel, (inner, count, query_tile,...  30.4 us
    unnamed x2, local copies, waits for them, and re-layouts  3.59 us

profile of v3, /device:TPU:0, one launch (start us, length us, event | category | flops | bytes accessed | tf_op | source)
XLA Modules:
  0.0 34.6 jit_solution(7402714763290694815)
XLA Ops:
  0.6 30.4 %layer_rows.1 = (bf16[16,512]{1,0:T(8,128)(2,1)}, bf16[1024,512]{1,0:T(8,128)(2,1)}) custom-call(s32[16,1024]{1,0:T(8,128)} %bitcast.2, s32[16,16]{1,0:T(8,128)} %hist_bins_hbm.1, s32[1,16]{1,0:T(1,128)} %bitcast.3, bf16[1024,512]{1,0:T(8,128)(2,1)} %table_hbm.1, bf16[512]{0:T(512)(128)(2,1)} %rank_vector_hbm.1, bf16[512,512]{1,0:T(8,128)(2,1)} %w_query_hbm.1, ...), custom_call_target="tpu_custom_call" | custom-call | tf_op jit(solution)/shard_map/layer_rows/pallas_call | solution.py:368
  31.0 1.3 %copy.15 = bf16[16,512]{1,0:T(8,128)(2,1)} copy(bf16[16,512]{1,0:T(8,128)(2,1)} %get-tuple-element.4) | data formatting | bytes 32768
  32.3 2.3 %copy.16 = bf16[1024,512]{1,0:T(8,128)(2,1)} copy(bf16[1024,512]{1,0:T(8,128)(2,1)} %get-tuple-element.5) | data formatting | bytes 2097152

commit v4 on v3

--- a/solution.py
+++ b/solution.py
@@ -12,6 +12,7 @@
 LANES = 128
 RADIX = 64
 VMEM_LIMIT = 64 << 20
+PIECES = 8
 epsilon = 1e-05
 F32 = jnp.float32
 BF16 = jnp.bfloat16
@@ -45,8 +46,7 @@
     w_out_hbm,
     w_up_hbm,
     w_down_hbm,
-    hist_out,
-    query_out,
+    gathered,
     query_bins,
     hist_bins,
     hist_ranks,
@@ -190,7 +190,7 @@
         queries_out[at, :] = dot(normalize(found).astype(BF16), w_query[...]).astype(BF16)
         return carry
 
-    lax.fori_loop(0, query_count // query_tile, query_step, 0, unroll=True)
+    lax.fori_loop(0, query_count // query_tile, query_step, 0)
 
     def finish(step, carry):
         copy_to(step).wait_send()
@@ -296,7 +296,7 @@
 
     def store(index):
         at = rows_at(index)
-        return pltpu.make_async_copy(results.at[at], query_out.at[at], store_sem.at[index])
+        return pltpu.make_async_copy(results.at[at], gathered.at[at], store_sem.at[index])
 
     first = slice(0, tile)
     project(first, [attend(first, pair) for pair in range(pairs)])
@@ -323,17 +323,27 @@
         result = result + feed(normed, part)
     result = result.astype(BF16)
     results[start:, :] = result
-    last = slice(start, query_count)
-    ending = [
-        pltpu.make_async_copy(results.at[last], query_out.at[last], store_sem.at[tiles - 1]),
-        pltpu.make_async_copy(results.at[query_count:], hist_out, store_sem.at[tiles]),
-    ]
-    for part in ending:
-        part.start()
-    for index in range(tiles - 1):
+    store(tiles - 1).start()
+    for index in range(tiles):
         store(index).wait()
-    for part in ending:
-        part.wait()
+
+
+def hand_out_kernel(results, hist_out, query_out, held, load_sem, store_sem):
+    query_count = query_out.shape[0]
+    piece = query_count // PIECES
+    loads, stores = [], []
+    for index in range(PIECES + 1):
+        at = slice(index * piece, (index + 1) * piece if index < PIECES else held.shape[0])
+        target = query_out.at[at] if index < PIECES else hist_out
+        loads.append(pltpu.make_async_copy(results.at[at], held.at[at], load_sem.at[index]))
+        stores.append(pltpu.make_async_copy(held.at[at], target, store_sem.at[index]))
+    for load in loads:
+        load.start()
+    for load, store in zip(loads, stores):
+        load.wait()
+        store.start()
+    for store in stores:
+        store.wait()
 
 
 def local(
@@ -365,17 +375,14 @@
         size for size in range(16, 257, 16) if row_count % size == 0 and size > own
     )
     hbm = pl.BlockSpec(memory_space=pltpu.HBM)
-    return pl.pallas_call(
+    results = pl.pallas_call(
         functools.partial(
             layer_kernel,
             (inner, count, query_tile, hist_tile, tile),
         ),
-        out_shape=(
-            jax.ShapeDtypeStruct((own, width), BF16),
-            jax.ShapeDtypeStruct((query_count, width), BF16),
-        ),
+        out_shape=jax.ShapeDtypeStruct((row_count, width), BF16),
         in_specs=[hbm] * 11,
-        out_specs=(hbm, hbm),
+        out_specs=hbm,
         scratch_shapes=[
             pltpu.VMEM((features, query_count), jnp.int32),
             pltpu.VMEM((own, features), jnp.int32),
@@ -420,6 +427,22 @@
         w_up,
         w_down,
     )
+    return pl.pallas_call(
+        hand_out_kernel,
+        out_shape=(
+            jax.ShapeDtypeStruct((own, width), BF16),
+            jax.ShapeDtypeStruct((query_count, width), BF16),
+        ),
+        in_specs=[hbm],
+        out_specs=(hbm, hbm),
+        scratch_shapes=[
+            pltpu.VMEM((row_count, width), BF16),
+            pltpu.SemaphoreType.DMA((PIECES + 1,)),
+            pltpu.SemaphoreType.DMA((PIECES + 1,)),
+        ],
+        compiler_params=pltpu.CompilerParams(vmem_limit_bytes=VMEM_LIMIT),
+        name="hand_out",
+    )(results)
 
 
 def solution(mesh):

time: 34.9 us -> 33.3 us (0.954)
  local copies, waits for them, and re-layouts: 3.59 us -> 0 us
  Pallas kernels: 30.4 us -> 32.4 us
    unnamed x2 -> x0, local copies, waits for them, and re-layouts: 3.59 us -> none
    pallas_call x0 -> x1, Pallas kernels: none -> 2.11 us  [local(): pl.pallas_call(hand_out_kernel, out_shape=(jax.ShapeDtypeStruct((own, wid...]
where the time goes in v4:
time: 33.3 us; the launch traced here: 33.1 us
  Pallas kernels  32.4 us (97%)
  between operations  0.64 us (2%)
    pallas_call x1, Pallas kernels, local(): pl.pallas_call(functools.partial(layer_kernel, (inner, count, query_tile,...  30.3 us
    pallas_call x1, Pallas kernels, local(): pl.pallas_call(hand_out_kernel, out_shape=(jax.ShapeDtypeStruct((own, wid...  2.11 us

profile of v4, /device:TPU:0, one launch (start us, length us, event | category | flops | bytes accessed | tf_op | source)
XLA Modules:
  0.0 33.1 jit_solution(13938792812480742279)
XLA Ops:
  0.6 30.3 %layer_rows.1.results = bf16[1040,512]{1,0:T(8,128)(2,1)} custom-call(s32[16,1024]{1,0:T(8,128)} %bitcast.2, s32[16,16]{1,0:T(8,128)} %hist_bins_hbm.1, s32[1,16]{1,0:T(1,128)} %bitcast.3, bf16[1024,512]{1,0:T(8,128)(2,1)} %table_hbm.1, bf16[512]{0:T(512)(128)(2,1)} %rank_vector_hbm.1, bf16[512,512]{1,0:T(8,128)(2,1)} %w_query_hbm.1, ...), custom_call_target="tpu_custom_call" | custom-call | tf_op jit(solution)/shard_map/layer_rows/pallas_call | solution.py:378
  31.0 2.1 %hand_out.1 = (bf16[16,512]{1,0:T(8,128)(2,1)}, bf16[1024,512]{1,0:T(8,128)(2,1)}) custom-call(bf16[1040,512]{1,0:T(8,128)(2,1)} %layer_rows.1.results), custom_call_target="tpu_custom_call" | custom-call | tf_op jit(solution)/shard_map/hand_out/pallas_call | solution.py:430
